TPU v7x, 32 devices: a whole 2x2x4 slice. The times are simulated.
32 devices in a mesh: seq: 8 (over y, x, core), pipe: 4 (over z).
Axes of the slice: x: 2, y: 2, z: 4, core: 2. Of those that a mesh axis runs over, the one named last changes fastest.
Arguments:
- query_in: bfloat16 [4, 1024, 4096], P('pipe', 'seq'), may hold values from -6 to 6
- key_in: bfloat16 [4, 1024, 4096], P('pipe', 'seq'), may hold values from -6 to 6
- value_in: bfloat16 [4, 1024, 4096], P('pipe', 'seq'), may hold values from -6 to 6
- grad_out: bfloat16 [4, 1024, 4096], P('pipe', 'seq'), may hold values from -6 to 6
- long_filter: float32 [4, 1024, 256], P('pipe', 'seq'), may hold values from -2 to 2, as said below
- short_taps: float32 [4, 3, 3, 4096], P('pipe'), may hold values from -3 to 3
Outputs:
- layer_out: bfloat16 [4, 1024, 4096], P('pipe', 'seq')
- passed_grads: bfloat16 [4, 3, 1024, 4096], P('pipe', None, 'seq')
- filter_grad: float32 [4, 1024, 256], P('pipe', 'seq')
- tap_grads: float32 [4, 3, 3, 4096], P('pipe')
Inputs may be any that keep to these rules, and one draw needn't show every extreme that they name: `long_filter`: one filter for each channel group of each section.
All inputs are finite; a program needn't handle non-finite values.
Results may differ from a plain program's by a relative error of at most 0.005.
Values may be sent and summed in bfloat16 or wider, within the bound.
No kernel may reach another device: no remote copies, remote signals or barrier semaphores. Data moves between devices by JAX's collectives and lax.ppermute only.
A program may use at most 256 MiB of HBM per device.

v0:
```python
import math
import jax
import jax.numpy as jnp
from jax import lax
from jax.sharding import PartitionSpec as P

exact_mode = lax.Precision.HIGHEST


def passed_along(x, axis, by):
    count = lax.axis_size(axis)
    pairs = [(i, i + by) for i in range(count) if 0 <= i + by < count]
    return lax.ppermute(x, axis, pairs)


def counting(length):
    return jnp.arange(length, dtype=jnp.int32)


def matmul(left, right):
    return jnp.dot(left, right, precision=exact_mode, preferred_element_type=jnp.float32)


def phases(row_index, col_index, modulus, direction):
    index_product = row_index[:, None] * col_index[None, :] % modulus
    phase_angle = index_product.astype(jnp.float32) * (-2.0 * math.pi * direction / modulus)
    return (jnp.cos(phase_angle), jnp.sin(phase_angle))


def complex_table(row_index, col_index, modulus, direction, factor):
    cosine_part, sine_part = phases(row_index, col_index, modulus, direction)
    upper = jnp.concatenate([cosine_part, -sine_part], axis=1)
    lower = jnp.concatenate([sine_part, cosine_part], axis=1)
    return jnp.concatenate([upper, lower], axis=0) * factor


def lead_segment(packed, row_index, col_index, modulus, direction, factor):
    in_shape = packed.shape
    flattened = packed.reshape(2 * in_shape[1], -1)
    table = complex_table(row_index, col_index, modulus, direction, factor)
    joined = matmul(table, flattened)
    return joined.reshape((2, row_index.shape[0]) + in_shape[2:])


def middle_segment(packed, row_index, col_index, modulus, direction):
    table = complex_table(row_index, col_index, modulus, direction, 1.0)
    table = table.reshape(2, row_index.shape[0], 2, col_index.shape[0])
    return jnp.einsum(
        "xrzb,zkbw->xkrw", table, packed, precision=exact_mode, preferred_element_type=jnp.float32
    )


def twiddle(packed, row_index, col_index, modulus, direction):
    cosine_part, sine_part = phases(row_index, col_index, modulus, direction)
    cosine_part = cosine_part[:, :, None]
    sine_part = sine_part[:, :, None]
    return jnp.stack(
        [
            packed[0] * cosine_part - packed[1] * sine_part,
            packed[0] * sine_part + packed[1] * cosine_part,
        ]
    )


def pack_pairs(values, pack_block):
    lead_dims = values.shape[:-1]
    split_view = values.reshape(lead_dims + (values.shape[-1] // (2 * pack_block), 2, pack_block))
    return jnp.stack(
        [
            split_view[..., 0, :].reshape(lead_dims + (-1,)),
            split_view[..., 1, :].reshape(lead_dims + (-1,)),
        ]
    )


def unpack_pairs(packed, pack_block):
    lead_dims = packed.shape[1:-1]
    pair_view = packed.reshape((2,) + lead_dims + (packed.shape[-1] // pack_block, pack_block))
    joined = jnp.stack([pair_view[0], pair_view[1]], axis=-2)
    return joined.reshape(lead_dims + (-1,))


def group_table(first_packed, col_count, half_group, groups):
    packed_index = first_packed + counting(col_count)
    return (packed_index[None, :] // half_group == counting(groups)[:, None]).astype(jnp.float32)


def spec_product(first_spec, second_spec):
    return jnp.stack(
        [
            first_spec[0] * second_spec[0] - first_spec[1] * second_spec[1],
            first_spec[0] * second_spec[1] + first_spec[1] * second_spec[0],
        ]
    )


def conj_product(first_spec, second_spec):
    return jnp.stack(
        [
            first_spec[0] * second_spec[0] + first_spec[1] * second_spec[1],
            first_spec[1] * second_spec[0] - first_spec[0] * second_spec[1],
        ]
    )


def spread_groups(spectrum, group_map):
    return jnp.einsum(
        "rktg,gq->rktq",
        spectrum,
        group_map,
        precision=exact_mode,
        preferred_element_type=jnp.float32,
    )


def sum_groups(spectrum, group_map):
    return jnp.einsum(
        "rktq,gq->rktg",
        spectrum,
        group_map,
        precision=exact_mode,
        preferred_element_type=jnp.float32,
    )


def local(query_in, key_in, value_in, grad_out, long_filter, short_taps):
    seq_size = lax.axis_size("seq")
    seq_rank = lax.axis_index("seq")
    rows_dev = query_in.shape[1]
    width = query_in.shape[2]
    groups = long_filter.shape[2]
    half_group = width // groups // 2
    pack_block = half_group // 2
    total_rows = rows_dev * seq_size
    fft_length = 2 * total_rows
    tap_table = short_taps[0]
    stacked_in = jnp.stack([query_in[0], key_in[0], value_in[0]])
    before = passed_along(stacked_in[:, rows_dev - 2 :, :], "seq", 1)
    extended = jnp.concatenate([before, stacked_in], axis=1).astype(jnp.float32)
    featured = tap_table[:, 0, None, :] * extended[:, 2 : 2 + rows_dev, :]
    featured = featured + tap_table[:, 1, None, :] * extended[:, 1 : 1 + rows_dev, :]
    featured = featured + tap_table[:, 2, None, :] * extended[:, 0:rows_dev, :]
    query_feat = featured[0]
    keyed = featured[1]
    valued = featured[2]
    grad_float = grad_out[0].astype(jnp.float32)
    product = (keyed * valued).astype(jnp.bfloat16)
    scaled = (grad_float * query_feat).astype(jnp.bfloat16)
    block_rows = rows_dev // seq_size
    group_map = group_table(0, width // 2, half_group, groups)
    freq_index = (
        (2 * seq_rank + counting(2))[:, None] + 2 * seq_size * counting(rows_dev)[None, :]
    ).reshape(-1)
    whole_filter = lax.all_gather(long_filter[0], "seq", axis=0, tiled=True)
    filter_cos, filter_sin = phases(freq_index, counting(total_rows), fft_length, 1)
    own_spec = jnp.stack(
        [matmul(filter_cos, whole_filter), matmul(filter_sin, whole_filter)]
    ).reshape(2, 2, rows_dev, groups)
    kernel = spread_groups(own_spec, group_map)

    def forward(signal):
        arrived = lax.all_to_all(signal[None], "seq", split_axis=1, concat_axis=0, tiled=True)
        packed = pack_pairs(arrived.astype(jnp.float32), pack_block)
        first_segment = lead_segment(
            packed, counting(2 * seq_size), counting(seq_size), 2 * seq_size, 1, 1.0
        )
        turned = twiddle(
            first_segment,
            counting(2 * seq_size),
            seq_rank * block_rows + counting(block_rows),
            fft_length,
            1,
        )
        gathered = lax.all_to_all(turned, "seq", split_axis=1, concat_axis=2, tiled=True)
        return middle_segment(gathered, counting(rows_dev), counting(rows_dev), rows_dev, 1)

    def inverse(spectrum):
        back_segment = middle_segment(
            spectrum, counting(rows_dev), counting(rows_dev), rows_dev, -1
        )
        turned = twiddle(
            back_segment, 2 * seq_rank + counting(2), counting(rows_dev), fft_length, -1
        )
        arrived = lax.all_to_all(turned, "seq", split_axis=2, concat_axis=1, tiled=True)
        row_data = lead_segment(
            arrived, counting(seq_size), counting(2 * seq_size), 2 * seq_size, -1, 1.0 / fft_length
        )
        spread_back = unpack_pairs(row_data, pack_block)
        return lax.all_to_all(spread_back, "seq", split_axis=0, concat_axis=1, tiled=True)[0]

    prod_spec = forward(product)
    conv_out = inverse(spec_product(prod_spec, kernel))
    scaled_spec = forward(scaled)
    back_out = inverse(conj_product(scaled_spec, kernel))
    cross_spec = sum_groups(conj_product(scaled_spec, prod_spec), group_map)
    cross_real = cross_spec[0].reshape(2 * rows_dev, groups)
    cross_imag = cross_spec[1].reshape(2 * rows_dev, groups)
    layer_out = (query_feat * conv_out).astype(jnp.bfloat16)
    grad_stack = jnp.stack([grad_float * conv_out, back_out * valued, back_out * keyed])
    after_rows = passed_along(grad_stack[:, :2, :].astype(jnp.bfloat16), "seq", -1).astype(
        jnp.float32
    )
    padded = jnp.concatenate([grad_stack, after_rows], axis=1)
    input_grads = tap_table[:, 0, None, :] * padded[:, 0:rows_dev, :]
    input_grads = input_grads + tap_table[:, 1, None, :] * padded[:, 1 : 1 + rows_dev, :]
    input_grads = input_grads + tap_table[:, 2, None, :] * padded[:, 2 : 2 + rows_dev, :]
    input_grads = input_grads.astype(jnp.bfloat16)
    tap_terms = jnp.stack(
        [
            jnp.sum(grad_stack * extended[:, 2 - tap_lag : 2 - tap_lag + rows_dev, :], axis=1)
            for tap_lag in range(3)
        ],
        axis=1,
    )
    tap_grads = lax.psum(tap_terms, "seq") / math.sqrt(total_rows)
    positions = counting(rows_dev * lax.axis_size("seq"))
    cosine_part, sine_part = phases(positions, freq_index, fft_length, -1)
    filter_grad = lax.psum_scatter(
        (matmul(cosine_part, cross_real) - matmul(sine_part, cross_imag)) / fft_length,
        "seq",
        scatter_dimension=0,
        tiled=True,
    ) / math.sqrt(total_rows * 2 * half_group)
    passed_grads = passed_along(input_grads, "pipe", -1)
    return (layer_out[None], passed_grads[None], filter_grad[None], tap_grads[None])


def solution(mesh):
    in_specs = (
        P("pipe", "seq", None),
        P("pipe", "seq", None),
        P("pipe", "seq", None),
        P("pipe", "seq", None),
        P("pipe", "seq", None),
        P("pipe", None, None, None),
    )
    out_specs = (
        P("pipe", "seq", None),
        P("pipe", None, "seq", None),
        P("pipe", "seq", None),
        P("pipe", None, None, None),
    )
    return jax.shard_map(local, mesh=mesh, in_specs=in_specs, out_specs=out_specs, check_vma=False)
```

profile of v0, /device:TPU:0, one launch (start us, length us, event | category | flops | bytes accessed | tf_op | source)
XLA Modules:
  0.0 850.4 jit_solution(6586171705041286776)
XLA Ops:
  20.4 7.1 reduce
  29.1 7.6 all-to-all-start.4
  36.9 15.1 %all-to-all-done.4 = bf16[8,2,32768]{2,1,0:T(2,128)(2,1)S(1)} async-done(((bf16[8,2,32768]{2,1,0:T(2,128)(2,1)}), bf16[8,2,32768]{2,1,0:T(2,128)(2,1)S(1)}, u32[]{:S(2)}, u32[]{:S(2)}) %all-to-all-start.4) | async-done | bytes 1048608 | tf_op jit(solution)/shard_map/all_to_all | solution.py:162
  57.9 8.5 reshape.367
  66.4 11.0 %fusion.148 = (f32[8,16,512,1,4]{1,0,4,3,2:T(8,128)}, f32[8,16,512,1,4]{1,0,4,3,2:T(8,128)}) fusion(f32[8,16,512,2,4]{1,0,4,3,2:T(8,128)} %reshape.367), kind=kLoop, calls=%fused_computation.231 | loop fusion | bytes 4194304 | tf_op jit(solution)/shard_map/slice | solution.py:70
  77.4 5.1 copy.183
  82.5 5.1 copy.184
  98.5 4.6 all-to-all-start.5
  105.5 39.8 %all-gather.3.cloned.1.call-done = f32[1,1024,256]{2,1,0:T(8,128)} async-done(((f32[1,128,256]{2,1,0:T(8,128)}), f32[1,1024,256]{2,1,0:T(8,128)}) %all-gather.3.cloned.1.call-update) | async-done | bytes 1048592 | tf_op jit(solution)/shard_map/all_gather | solution.py:154
  145.4 6.3 fusion.49
  151.7 6.7 fusion.51
  164.6 7.1 fusion.18
  179.9 7.3 copy.194
  187.3 6.0 all-to-all-start.6
  193.3 49.7 %all-to-all-done.6 = f32[2,2,128,2048]{3,0,1,2:T(2,128)} async-done(((f32[2,2,128,2048]{3,0,1,2:T(2,128)}), f32[2,2,128,2048]{3,0,1,2:T(2,128)}, u32[]{:S(2)}, u32[]{:S(2)}) %all-to-all-start.6) | async-done | bytes 4194336 | tf_op jit(solution)/shard_map/all_to_all | solution.py:184
  243.1 4.6 copy.195
  252.9 8.8 %copy.197 = f32[8,32768]{0,1:T(8,128)} copy(f32[8,32768]{1,0:T(8,128)S(1)} %get-tuple-element.37) | data formatting | bytes 2097152 | tf_op jit(solution)/shard_map/slice | solution.py:79
  261.7 8.8 %copy.198 = f32[8,32768]{0,1:T(8,128)} copy(f32[8,32768]{1,0:T(8,128)S(1)} %get-tuple-element.38) | data formatting | bytes 2097152 | tf_op jit(solution)/shard_map/slice | solution.py:79
  270.6 23.0 %pad_maximum_fusion.1 = f32[8,16,512,2,4]{0,4,2,1,3:T(4,128)} fusion(f32[8,16,512,1,4]{0,4,2,1,3:T(4,128)} %bitcast.249, f32[8,16,512,1,4]{0,4,2,1,3:T(4,128)} %bitcast.247), kind=kLoop, calls=%fused_computation.1 | loop fusion | flops 524288 | bytes 4194304 | tf_op jit(solution)/shard_map/stack | solution.py:79
  293.6 30.4 %copy.199 = f32[8,16,512,2,4]{1,0,4,3,2:T(8,128)} copy(f32[8,16,512,2,4]{0,4,2,1,3:T(4,128)} %pad_maximum_fusion.1) | data formatting | bytes 4194304 | tf_op jit(solution)/shard_map/stack | solution.py:79
  324.0 9.6 %copy.200 = f32[8,16,4096]{2,1,0:T(8,128)S(1)} copy(f32[8,16,4096]{1,0,2:T(8,128)} %bitcast.245) | data formatting | bytes 4194304 | tf_op jit(solution)/shard_map/reshape | solution.py:80
  333.6 29.4 %all_to_all.102 = f32[8,16,4096]{2,1,0:T(8,128)S(1)} all-to-all(f32[8,16,4096]{2,1,0:T(8,128)S(1)} %copy.200), channel_id=1, replica_groups=mesh['seq'=8,'pipe'=4] {'seq'}, dimensions={0} | all-to-all | bytes 4194304 | tf_op jit(solution)/shard_map/all_to_all | solution.py:189
  370.7 8.4 reduce.1
  380.7 18.8 %all_to_all.103 = bf16[8,2,32768]{2,1,0:T(2,128)(2,1)S(1)} all-to-all(bf16[8,2,32768]{2,1,0:T(2,128)(2,1)} %reshape.382), channel_id=1, replica_groups=mesh['seq'=8,'pipe'=4] {'seq'}, dimensions={0} | all-to-all | bytes 2097152 | tf_op jit(solution)/shard_map/all_to_all | solution.py:162
  403.0 4.6 copy_convert_fusion.1
  410.5 10.6 %reshape.366 = f32[8,16,512,2,4]{1,0,4,3,2:T(8,128)} reshape(f32[1,128,4096]{1,2,0:T(8,128)} %copy.159) | data formatting | bytes 4194304 | tf_op jit(solution)/shard_map/convert_element_type | solution.py:163
  421.0 11.0 %fusion.149 = (f32[8,16,512,1,4]{1,0,4,3,2:T(8,128)}, f32[8,16,512,1,4]{1,0,4,3,2:T(8,128)}) fusion(f32[8,16,512,2,4]{1,0,4,3,2:T(8,128)} %reshape.366), kind=kLoop, calls=%fused_computation.232 | loop fusion | bytes 4194304 | tf_op jit(solution)/shard_map/slice | solution.py:70
  432.1 5.1 copy.160
  437.2 6.2 copy.161
  453.6 51.9 %all_to_all.104 = f32[2,16,16,2048]{3,2,0,1:T(8,128)S(1)} all-to-all(f32[2,16,16,2048]{3,2,0,1:T(8,128)S(1)} %pad_maximum_fusion.4), channel_id=1, replica_groups=mesh['seq'=8,'pipe'=4] {'seq'}, dimensions={1} | all-to-all | bytes 8388608 | tf_op jit(solution)/shard_map/all_to_all | solution.py:174
  506.5 8.3 fusion.15
  514.8 5.4 multiply_add_fusion.1
  520.2 5.1 fusion.22
  528.0 7.3 copy.173
  535.3 52.8 %all_to_all.105 = f32[2,2,128,2048]{3,0,1,2:T(2,128)S(1)} all-to-all(f32[2,2,128,2048]{3,0,1,2:T(2,128)} %copy.173), channel_id=1, replica_groups=mesh['seq'=8,'pipe'=4] {'seq'}, dimensions={2} | all-to-all | bytes 8388608 | tf_op jit(solution)/shard_map/all_to_all | solution.py:184
  596.7 9.1 %copy.176 = f32[8,32768]{0,1:T(8,128)} copy(f32[8,32768]{1,0:T(8,128)} %get-tuple-element.39) | data formatting | bytes 2097152 | tf_op jit(solution)/shard_map/slice | solution.py:79
  605.8 8.8 %copy.177 = f32[8,32768]{0,1:T(8,128)} copy(f32[8,32768]{1,0:T(8,128)S(1)} %get-tuple-element.40) | data formatting | bytes 2097152 | tf_op jit(solution)/shard_map/slice | solution.py:79
  614.7 23.0 %pad_maximum_fusion = f32[8,16,512,2,4]{0,4,2,1,3:T(4,128)} fusion(f32[8,16,512,1,4]{0,4,2,1,3:T(4,128)} %bitcast.250, f32[8,16,512,1,4]{0,4,2,1,3:T(4,128)} %bitcast.248), kind=kLoop, calls=%fused_computation | loop fusion | flops 524288 | bytes 4194304 | tf_op jit(solution)/shard_map/stack | solution.py:79
  637.7 30.4 %copy.178 = f32[8,16,512,2,4]{1,0,4,3,2:T(8,128)} copy(f32[8,16,512,2,4]{0,4,2,1,3:T(4,128)} %pad_maximum_fusion) | data formatting | bytes 4194304 | tf_op jit(solution)/shard_map/stack | solution.py:79
  668.1 10.6 %copy.179 = f32[8,16,4096]{2,1,0:T(8,128)} copy(f32[8,16,4096]{1,0,2:T(8,128)} %bitcast.246) | data formatting | bytes 4194304 | tf_op jit(solution)/shard_map/reshape | solution.py:80
  678.7 4.5 all-to-all-start.3
  683.5 6.6 fusion.9
  690.1 19.8 %all-to-all-done.3 = f32[8,16,4096]{2,1,0:T(8,128)} async-done(((f32[8,16,4096]{2,1,0:T(8,128)}), f32[8,16,4096]{2,1,0:T(8,128)}, u32[]{:S(2)}, u32[]{:S(2)}) %all-to-all-start.3) | async-done | bytes 2097184 | tf_op jit(solution)/shard_map/all_to_all | solution.py:189
  720.9 9.4 %multiply_reduce_fusion.2 = (f32[3,4096]{1,0:T(4,128)S(1)}, f32[3,4096]{1,0:T(4,128)S(1)}, f32[3,4096]{1,0:T(4,128)S(1)}, bf16[3,128,4096]{2,1,0:T(8,128)(2,1)}) fusion(f32[3,130,4096]{2,1,0:T(8,128)S(1)} %bitcast.244, f32[1,128,4096]{2,1,0:T(8,128)} %get-tuple-element.14, f32[1,128,4096]{2,1,0:T(8,128)S(1)} %get-tuple-element.13, ...), kind=kLoop, calls=%fused_computation.11 | loop fusion | flops 21983232 | bytes 41189376 | tf_op jit(solution)/shard_map/reduce_sum | solution.py:210
  732.0 5.7 fusion.54
  737.7 6.2 fusion.42
  745.0 38.3 %reduce-scatter.2.cloned.1.call-done = f32[128,256]{1,0:T(8,128)} async-done(((f32[1024,256]{1,0:T(8,128)}), f32[128,256]{1,0:T(8,128)}) %reduce-scatter.2.cloned.1.call-update) | async-done | bytes 131088 | tf_op jit(solution)/shard_map/reduce_scatter | solution.py:218
  784.8 55.2 %all-reduce.2.cloned.1.call-done = f32[3,3,4096]{2,1,0:T(4,128)} async-done(((f32[3,3,4096]{2,1,0:T(4,128)}), f32[3,3,4096]{2,1,0:T(4,128)}) %all-reduce.2.cloned.1.call-update) | async-done | bytes 147472 | tf_op jit(solution)/shard_map/psum | solution.py:215
  (165 shorter events, 110.4 us)
Async XLA Ops:
  7.2 2.7 copy-start.14
  7.2 5.3 copy-start.23
  10.0 3.3 collective-permute-start
  12.8 1.5 copy-start.15
  12.8 1.5 copy-start.17
  12.8 1.5 copy-start.19
  14.3 2.8 copy-start
  14.3 2.7 copy-start.8
  17.0 2.8 copy-start.5
  29.1 22.9 %all-to-all-start.4 = ((bf16[8,2,32768]{2,1,0:T(2,128)(2,1)}), bf16[8,2,32768]{2,1,0:T(2,128)(2,1)S(1)}, u32[]{:S(2)}, u32[]{:S(2)}) async-start(bf16[8,2,32768]{2,1,0:T(2,128)(2,1)} %reshape.384), calls=%async_computation.4 | async-start | bytes 2097152 | tf_op jit(solution)/shard_map/all_to_all | solution.py:162
  98.5 63.6 %all-to-all-start.5 = ((f32[2,16,16,2048]{3,2,0,1:T(8,128)}), f32[2,16,16,2048]{3,2,0,1:T(8,128)}, u32[]{:S(2)}, u32[]{:S(2)}) async-start(f32[2,16,16,2048]{3,2,0,1:T(8,128)} %pad_maximum_fusion.6), calls=%async_computation.5 | async-start | bytes 8388608 | tf_op jit(solution)/shard_map/all_to_all | solution.py:174
  103.1 42.3 %all-gather.3.cloned.1.call-start = ((), (), s32[]{:S(2)}) async-start(), calls=%async_computation.11 | async-start | bytes 1179648 | tf_op jit(solution)/shard_map/all_gather | solution.py:154
  104.6 60.0 %copy-start.10 = (f32[2,128,2,128]{3,2,1,0:T(2,128)}, f32[2,128,2,128]{3,2,1,0:T(2,128)S(1)}, u32[]{:S(2)}) copy-start(f32[2,128,2,128]{3,2,1,0:T(2,128)S(1)} %reshape.359) | copy-start | bytes 786436
  105.3 68.5 %copy-start.12 = (f32[2,128,2,128]{3,2,1,0:T(2,128)}, f32[2,128,2,128]{3,2,1,0:T(2,128)S(1)}, u32[]{:S(2)}) copy-start(f32[2,128,2,128]{3,2,1,0:T(2,128)S(1)} %reshape.360) | copy-start | bytes 786436
  105.3 53.1 %copy-start.24 = (s32[2048]{0:T(1024)}, s32[2048]{0:T(1024)S(1)}, u32[]{:S(2)}) copy-start(s32[2048]{0:T(1024)S(1)} %add_select_fusion.3) | copy-start | bytes 24580
  105.4 53.0 %copy-start.26 = (s32[256]{0:T(256)}, s32[256]{0:T(256)S(1)}, u32[]{:S(2)}) copy-start(s32[256]{0:T(256)S(1)} %add_bitcast_fusion) | copy-start | bytes 3076
  145.4 6.3 copy-start.28
  164.6 7.1 copy-start.1
  171.7 2.0 copy-start.3
  187.3 55.8 %all-to-all-start.6 = ((f32[2,2,128,2048]{3,0,1,2:T(2,128)}), f32[2,2,128,2048]{3,0,1,2:T(2,128)}, u32[]{:S(2)}, u32[]{:S(2)}) async-start(f32[2,2,128,2048]{3,0,1,2:T(2,128)} %copy.194), calls=%async_computation.6 | async-start | bytes 8388608 | tf_op jit(solution)/shard_map/all_to_all | solution.py:184
  505.6 1.0 copy-start.11
  506.5 8.3 copy-start.2
  506.5 8.3 copy-start.4
  514.8 5.4 copy-start.13
  678.7 4.8 copy-start.25
  678.7 31.1 %all-to-all-start.3 = ((f32[8,16,4096]{2,1,0:T(8,128)}), f32[8,16,4096]{2,1,0:T(8,128)}, u32[]{:S(2)}, u32[]{:S(2)}) async-start(f32[8,16,4096]{2,1,0:T(8,128)} %copy.179), calls=%async_computation.3 | async-start | bytes 4194304 | tf_op jit(solution)/shard_map/all_to_all | solution.py:189
  683.2 100.1 %reduce-scatter.2.cloned.1.call-start = ((), (), s32[]{:S(2)}) async-start(), calls=%async_computation.9 | async-start | bytes 1179648 | tf_op jit(solution)/shard_map/reduce_scatter | solution.py:218
  683.5 26.4 %copy-start.9 = (bf16[1,128,4096]{2,1,0:T(8,128)(2,1)S(1)}, bf16[1,128,4096]{2,1,0:T(8,128)(2,1)}, u32[]{:S(2)}) copy-start(bf16[1,128,4096]{2,1,0:T(8,128)(2,1)} %param.9) | copy-start | bytes 3145732
  709.8 3.8 copy-start.6
  713.6 4.2 copy-start.7
  713.6 2.3 copy-start.21
  713.6 7.3 slice-start
  714.3 3.4 collective-permute-start.1
  717.8 3.1 slice-start.1
  717.8 3.1 copy-start.16
  717.8 3.1 copy-start.18
  717.8 3.1 copy-start.20
  720.9 11.1 %copy-start.27 = (s32[256]{0:T(256)S(1)}, s32[256]{0:T(256)}, u32[]{:S(2)}) copy-start(s32[256]{0:T(256)} %copy-done.26) | copy-start | bytes 3076
  730.3 7.4 copy-start.22
  730.3 111.5 %collective-permute-start.2 = (bf16[3,128,4096]{2,1,0:T(8,128)(2,1)}, bf16[3,128,4096]{2,1,0:T(8,128)(2,1)S(1)}, u32[]{:S(2)}, u32[]{:S(2)}) collective-permute-start(bf16[3,128,4096]{2,1,0:T(8,128)(2,1)} %get-tuple-element.19), channel_id=1, source_target_pairs={{1,0},{2,1},{3,2},{5,4},{6,5},{7,6},{9,8},{10,9},{11,10},{13,12},{... | collective-permute-start | bytes 9437192 | tf_op jit(solution)/shard_map/ppermute | solution.py:13
  743.9 96.1 %all-reduce.2.cloned.1.call-start = ((), (), s32[]{:S(2)}) async-start(), calls=%async_computation.10 | async-start | bytes 393216 | tf_op jit(solution)/shard_map/psum | solution.py:215
Sparse Core Ops, SparseCore 0:
  105.8 39.5 all-gather.2
  744.0 39.1 reduce-scatter.1
  786.3 53.6 all-reduce.1
where the time goes:
time: 862 us; the launch traced here: 850 us
  local copies, waits for them, and re-layouts  248 us (29%)
  waiting for transfers between devices  220 us (26%)
  blocking collectives  153 us (18%)
  other arithmetic  116 us (13%)
  matrix products  70.2 us (8%)
  starting transfers between devices  29 us (3%)
  between operations  15.1 us (2%)
    another operation x2, local copies, waits for them, and re-layouts, unpack_pairs(): joined = jnp.stack([pair_view[0], pair_view[1]], axis=-2)  60.9 us
    psum x1, waiting for transfers between devices, local(): tap_grads = lax.psum(tap_terms, 'seq') / math.sqrt(total_rows)  55.2 us
    all_to_all x1, blocking collectives, inverse(): lax.all_to_all(turned, 'seq', split_axis=2, concat_axis=1, tiled=True)  52.8 us
    all_to_all x1, blocking collectives, forward(): lax.all_to_all(turned, 'seq', split_axis=1, concat_axis=2, tiled=True)  51.9 us
    all_to_all x1, waiting for transfers between devices, inverse(): lax.all_to_all(turned, 'seq', split_axis=2, concat_axis=1, tiled=True)  49.7 us
    another operation x2, other arithmetic, unpack_pairs(): joined = jnp.stack([pair_view[0], pair_view[1]], axis=-2)  46 us
    all_gather x1, waiting for transfers between devices, local(): whole_filter = lax.all_gather(long_filter[0], 'seq', axis=0, tiled=True)  39.8 us
    reduce_scatter x1, waiting for transfers between devices, local(): lax.psum_scatter((matmul(cosine_part, cross_real) - matmul(sine_part, cro...  38.3 us
  transfers between devices with their start and end apart: 10, of which 8 were waited for; matrix products, arithmetic and copies ran while one was open for 5% of the time, Pallas kernels for 0%

commit v1 on v0

--- a/solution.py
+++ b/solution.py
@@ -212,7 +212,7 @@
         ],
         axis=1,
     )
-    tap_grads = lax.psum(tap_terms, "seq") / math.sqrt(total_rows)
+    tap_grads = jnp.sum(lax.all_gather(tap_terms, "seq"), axis=0) / math.sqrt(total_rows)
     positions = counting(rows_dev * lax.axis_size("seq"))
     cosine_part, sine_part = phases(positions, freq_index, fft_length, -1)
     filter_grad = lax.psum_scatter(

time: 862 us -> 833 us (0.966)
  waiting for transfers between devices: 220 us -> 186 us
    psum x1 -> x0, waiting for transfers between devices: 55.2 us -> none  [local(): tap_grads = lax.psum(tap_terms, 'seq') / math.sqrt(total_rows)]
    all_gather x0 -> x1, waiting for transfers between devices: none -> 25.9 us  [local(): lax.all_gather(tap_terms, 'seq')]
    ppermute x3, waiting for transfers between devices: 1.45 us -> 23.3 us  [passed_along(): return lax.ppermute(x, axis, pairs)]
    reduce_scatter x1, waiting for transfers between devices: 38.3 us -> 17.9 us  [local(): lax.psum_scatter((matmul(cosine_part, cross_real) - matmul(sine_part, cro...]
    unnamed x81 -> x80, local copies, waits for them, and re-layouts: 28.1 us -> 30.4 us
  transfers between devices with their start and end apart: 10 -> 10, of which waited for: 8 -> 8; matrix products, arithmetic and copies ran while one was open for 5% -> 7% of each run, Pallas kernels for 0% -> 0%
where the time goes in v1:
time: 833 us; the launch traced here: 821 us
  local copies, waits for them, and re-layouts  249 us (30%)
  waiting for transfers between devices  186 us (22%)
  blocking collectives  153 us (18%)
  other arithmetic  119 us (14%)
  matrix products  70 us (8%)
  starting transfers between devices  28.1 us (3%)
  between operations  15.1 us (2%)
    another operation x2, local copies, waits for them, and re-layouts, unpack_pairs(): joined = jnp.stack([pair_view[0], pair_view[1]], axis=-2)  60.9 us
    all_to_all x1, blocking collectives, inverse(): lax.all_to_all(turned, 'seq', split_axis=2, concat_axis=1, tiled=True)  52.9 us
    all_to_all x1, blocking collectives, forward(): lax.all_to_all(turned, 'seq', split_axis=1, concat_axis=2, tiled=True)  51.7 us
    all_to_all x1, waiting for transfers between devices, inverse(): lax.all_to_all(turned, 'seq', split_axis=2, concat_axis=1, tiled=True)  49.5 us
    another operation x2, other arithmetic, unpack_pairs(): joined = jnp.stack([pair_view[0], pair_view[1]], axis=-2)  46 us
    all_gather x1, waiting for transfers between devices, local(): whole_filter = lax.all_gather(long_filter[0], 'seq', axis=0, tiled=True)  39.8 us
    slice x6, local copies, waits for them, and re-layouts, unpack_pairs(): joined = jnp.stack([pair_view[0], pair_view[1]], axis=-2)  36.9 us
    dot_general x8, matrix products, matmul(): jnp.dot(left, right, precision=exact_mode, preferred_element_type=jnp.flo...  36.5 us
  transfers between devices with their start and end apart: 10, of which 8 were waited for; matrix products, arithmetic and copies ran while one was open for 7% of the time, Pallas kernels for 0%

profile of v1, /device:TPU:0, one launch (start us, length us, event | category | flops | bytes accessed | tf_op | source)
XLA Modules:
  0.0 820.7 jit_solution(14462549419644305200)
XLA Ops:
  20.4 7.0 reduce
  29.0 7.5 all-to-all-start.4
  36.8 15.1 %all-to-all-done.4 = bf16[8,2,32768]{2,1,0:T(2,128)(2,1)S(1)} async-done(((bf16[8,2,32768]{2,1,0:T(2,128)(2,1)}), bf16[8,2,32768]{2,1,0:T(2,128)(2,1)S(1)}, u32[]{:S(2)}, u32[]{:S(2)}) %all-to-all-start.4) | async-done | bytes 1048608 | tf_op jit(solution)/shard_map/all_to_all | solution.py:162
  57.9 8.5 %reshape.376 = f32[8,16,512,2,4]{1,0,4,3,2:T(8,128)} reshape(f32[1,128,4096]{1,2,0:T(8,128)S(1)} %copy.186) | data formatting | bytes 4194304 | tf_op jit(solution)/shard_map/convert_element_type | solution.py:163
  66.4 11.0 %fusion.149 = (f32[8,16,512,1,4]{1,0,4,3,2:T(8,128)}, f32[8,16,512,1,4]{1,0,4,3,2:T(8,128)}) fusion(f32[8,16,512,2,4]{1,0,4,3,2:T(8,128)} %reshape.376), kind=kLoop, calls=%fused_computation.232 | loop fusion | bytes 4194304 | tf_op jit(solution)/shard_map/slice | solution.py:70
  77.4 5.1 copy.187
  82.5 5.1 copy.188
  105.5 39.8 %all-gather.5.cloned.1.call-done = f32[1,1024,256]{2,1,0:T(8,128)} async-done(((f32[1,128,256]{2,1,0:T(8,128)}), f32[1,1024,256]{2,1,0:T(8,128)}) %all-gather.5.cloned.1.call-update) | async-done | bytes 1048592 | tf_op jit(solution)/shard_map/all_gather | solution.py:154
  145.3 6.3 fusion.49
  151.6 6.7 fusion.51
  164.7 7.1 fusion.18
  180.1 7.3 copy.198
  187.4 6.0 all-to-all-start.6
  193.4 49.5 %all-to-all-done.6 = f32[2,2,128,2048]{3,0,1,2:T(2,128)} async-done(((f32[2,2,128,2048]{3,0,1,2:T(2,128)}), f32[2,2,128,2048]{3,0,1,2:T(2,128)}, u32[]{:S(2)}, u32[]{:S(2)}) %all-to-all-start.6) | async-done | bytes 4194336 | tf_op jit(solution)/shard_map/all_to_all | solution.py:184
  242.9 4.6 copy.199
  252.7 8.9 %copy.201 = f32[8,32768]{0,1:T(8,128)} copy(f32[8,32768]{1,0:T(8,128)S(1)} %get-tuple-element.49) | data formatting | bytes 2097152 | tf_op jit(solution)/shard_map/slice | solution.py:79
  261.6 8.8 %copy.202 = f32[8,32768]{0,1:T(8,128)} copy(f32[8,32768]{1,0:T(8,128)S(1)} %get-tuple-element.50) | data formatting | bytes 2097152 | tf_op jit(solution)/shard_map/slice | solution.py:79
  270.4 23.0 %pad_maximum_fusion.1 = f32[8,16,512,2,4]{0,4,2,1,3:T(4,128)} fusion(f32[8,16,512,1,4]{0,4,2,1,3:T(4,128)} %bitcast.252, f32[8,16,512,1,4]{0,4,2,1,3:T(4,128)} %bitcast.250), kind=kLoop, calls=%fused_computation.1 | loop fusion | flops 524288 | bytes 4194304 | tf_op jit(solution)/shard_map/stack | solution.py:79
  293.4 30.4 %copy.203 = f32[8,16,512,2,4]{1,0,4,3,2:T(8,128)} copy(f32[8,16,512,2,4]{0,4,2,1,3:T(4,128)} %pad_maximum_fusion.1) | data formatting | bytes 4194304 | tf_op jit(solution)/shard_map/stack | solution.py:79
  323.9 9.6 %copy.204 = f32[8,16,4096]{2,1,0:T(8,128)S(1)} copy(f32[8,16,4096]{1,0,2:T(8,128)} %bitcast.248) | data formatting | bytes 4194304 | tf_op jit(solution)/shard_map/reshape | solution.py:80
  333.5 29.4 %all_to_all.102 = f32[8,16,4096]{2,1,0:T(8,128)S(1)} all-to-all(f32[8,16,4096]{2,1,0:T(8,128)S(1)} %copy.204), channel_id=1, replica_groups=mesh['seq'=8,'pipe'=4] {'seq'}, dimensions={0} | all-to-all | bytes 4194304 | tf_op jit(solution)/shard_map/all_to_all | solution.py:189
  370.6 8.4 %reduce.1 = bf16[128,4096]{1,0:T(8,128)(2,1)S(1)} reduce(bf16[128,1,4096]{2,1,0:T(2,128)(2,1)} %bitcast.270, bf16[]{:T(256)} %broadcast.427), dimensions={1}, to_apply=%bitcast.239.reduce_sub_computation | reduce | bytes 2097154
  380.6 18.8 %all_to_all.103 = bf16[8,2,32768]{2,1,0:T(2,128)(2,1)S(1)} all-to-all(bf16[8,2,32768]{2,1,0:T(2,128)(2,1)} %reshape.392), channel_id=1, replica_groups=mesh['seq'=8,'pipe'=4] {'seq'}, dimensions={0} | all-to-all | bytes 2097152 | tf_op jit(solution)/shard_map/all_to_all | solution.py:162
  402.9 4.6 copy_convert_fusion.1
  410.3 10.6 %reshape.375 = f32[8,16,512,2,4]{1,0,4,3,2:T(8,128)} reshape(f32[1,128,4096]{1,2,0:T(8,128)} %copy.163) | data formatting | bytes 4194304 | tf_op jit(solution)/shard_map/convert_element_type | solution.py:163
  420.9 11.0 %fusion.150 = (f32[8,16,512,1,4]{1,0,4,3,2:T(8,128)}, f32[8,16,512,1,4]{1,0,4,3,2:T(8,128)}) fusion(f32[8,16,512,2,4]{1,0,4,3,2:T(8,128)} %reshape.375), kind=kLoop, calls=%fused_computation.233 | loop fusion | bytes 4194304 | tf_op jit(solution)/shard_map/slice | solution.py:70
  431.9 5.1 copy.164
  437.0 6.4 copy.165
  453.7 51.7 %all_to_all.104 = f32[2,16,16,2048]{3,2,0,1:T(8,128)S(1)} all-to-all(f32[2,16,16,2048]{3,2,0,1:T(8,128)S(1)} %pad_maximum_fusion.4), channel_id=1, replica_groups=mesh['seq'=8,'pipe'=4] {'seq'}, dimensions={1} | all-to-all | bytes 8388608 | tf_op jit(solution)/shard_map/all_to_all | solution.py:174
  505.9 8.3 %fusion.15 = f32[2,2,128,2048]{2,3,0,1:T(8,128)} fusion(f32[2,2,128,2048,1]{3,2,1,0,4:T(8,128)S(1)} %bitcast.260, f32[2,128,2,128]{3,2,1,0:T(2,128)S(1)} %reshape.368), kind=kOutput, calls=%fused_computation.33 | convolution fusion | flops 3221225472 | bytes 8650752 | tf_op jit(solution)/shard_map/xrzb,zkbw->xkrw/dot_general | solution.py:48
  514.2 5.4 multiply_add_fusion.1
  519.6 5.1 fusion.22
  527.3 7.4 copy.177
  534.7 52.9 %all_to_all.105 = f32[2,2,128,2048]{3,0,1,2:T(2,128)S(1)} all-to-all(f32[2,2,128,2048]{3,0,1,2:T(2,128)} %copy.177), channel_id=1, replica_groups=mesh['seq'=8,'pipe'=4] {'seq'}, dimensions={2} | all-to-all | bytes 8388608 | tf_op jit(solution)/shard_map/all_to_all | solution.py:184
  596.1 9.1 %copy.180 = f32[8,32768]{0,1:T(8,128)} copy(f32[8,32768]{1,0:T(8,128)} %get-tuple-element.51) | data formatting | bytes 2097152 | tf_op jit(solution)/shard_map/slice | solution.py:79
  605.3 8.8 %copy.181 = f32[8,32768]{0,1:T(8,128)} copy(f32[8,32768]{1,0:T(8,128)S(1)} %get-tuple-element.52) | data formatting | bytes 2097152 | tf_op jit(solution)/shard_map/slice | solution.py:79
  614.1 23.0 %pad_maximum_fusion = f32[8,16,512,2,4]{0,4,2,1,3:T(4,128)} fusion(f32[8,16,512,1,4]{0,4,2,1,3:T(4,128)} %bitcast.253, f32[8,16,512,1,4]{0,4,2,1,3:T(4,128)} %bitcast.251), kind=kLoop, calls=%fused_computation | loop fusion | flops 524288 | bytes 4194304 | tf_op jit(solution)/shard_map/stack | solution.py:79
  637.1 30.4 %copy.182 = f32[8,16,512,2,4]{1,0,4,3,2:T(8,128)} copy(f32[8,16,512,2,4]{0,4,2,1,3:T(4,128)} %pad_maximum_fusion) | data formatting | bytes 4194304 | tf_op jit(solution)/shard_map/stack | solution.py:79
  667.5 10.6 %copy.183 = f32[8,16,4096]{2,1,0:T(8,128)} copy(f32[8,16,4096]{1,0,2:T(8,128)} %bitcast.249) | data formatting | bytes 4194304 | tf_op jit(solution)/shard_map/reshape | solution.py:80
  682.9 5.7 fusion.9
  688.7 6.2 fusion.54
  694.9 14.4 %all-to-all-done.3 = f32[8,16,4096]{2,1,0:T(8,128)} async-done(((f32[8,16,4096]{2,1,0:T(8,128)}), f32[8,16,4096]{2,1,0:T(8,128)}, u32[]{:S(2)}, u32[]{:S(2)}) %all-to-all-start.3) | async-done | bytes 2097184 | tf_op jit(solution)/shard_map/all_to_all | solution.py:189
  715.7 6.2 fusion.42
  722.1 5.8 pad_maximum_fusion.2
  729.2 9.8 %multiply_reduce_fusion.2 = (f32[3,4096]{1,0:T(4,128)S(1)}, f32[3,4096]{1,0:T(4,128)S(1)}, f32[3,4096]{1,0:T(4,128)S(1)}, bf16[3,128,4096]{2,1,0:T(8,128)(2,1)}) fusion(f32[3,130,4096]{2,1,0:T(8,128)S(1)} %bitcast.247, f32[1,128,4096]{2,1,0:T(8,128)} %get-tuple-element.26, f32[1,128,4096]{2,1,0:T(8,128)S(1)} %copy-done.7, f32[1,128,4096]{2,1,0:T(8,128)} %copy-done.9, ...), kind=kLoop, calls=%fused_computation.11 | loop fusion | flops 21983232 | bytes 41189376 | tf_op jit(solution)/shard_map/reduce_sum | solution.py:210
  741.2 17.9 %reduce-scatter.2.cloned.1.call-done = f32[128,256]{1,0:T(8,128)} async-done(((f32[1024,256]{1,0:T(8,128)}), f32[128,256]{1,0:T(8,128)}) %reduce-scatter.2.cloned.1.call-update) | async-done | bytes 131088 | tf_op jit(solution)/shard_map/reduce_scatter | solution.py:218
  760.7 25.9 %all-gather.7.cloned.1.call-done = f32[24,3,4096]{2,1,0:T(4,128)} async-done(((f32[3,3,4096]{2,1,0:T(4,128)}), f32[24,3,4096]{2,1,0:T(4,128)}) %all-gather.7.cloned.1.call-update) | async-done | bytes 1179664 | tf_op jit(solution)/shard_map/all_gather | solution.py:215
  789.3 22.8 %collective-permute-done.2 = bf16[3,128,4096]{2,1,0:T(8,128)(2,1)S(1)} collective-permute-done((bf16[3,128,4096]{2,1,0:T(8,128)(2,1)}, bf16[3,128,4096]{2,1,0:T(8,128)(2,1)S(1)}, u32[]{:S(2)}, u32[]{:S(2)}) %collective-permute-start.2) | collective-permute-done | bytes 3145760 | tf_op jit(solution)/shard_map/ppermute | solution.py:13
  (164 shorter events, 116.5 us)
Async XLA Ops:
  7.2 2.7 copy-start.14
  7.2 5.3 copy-start.21
  10.0 3.3 collective-permute-start
  12.8 1.5 copy-start.15
  12.8 1.5 copy-start.17
  12.8 1.5 copy-start.19
  14.3 2.7 copy-start
  14.3 2.7 copy-start.10
  17.0 2.8 copy-start.5
  29.0 22.9 %all-to-all-start.4 = ((bf16[8,2,32768]{2,1,0:T(2,128)(2,1)}), bf16[8,2,32768]{2,1,0:T(2,128)(2,1)S(1)}, u32[]{:S(2)}, u32[]{:S(2)}) async-start(bf16[8,2,32768]{2,1,0:T(2,128)(2,1)} %reshape.394), calls=%async_computation.4 | async-start | bytes 2097152 | tf_op jit(solution)/shard_map/all_to_all | solution.py:162
  98.5 63.8 %all-to-all-start.5 = ((f32[2,16,16,2048]{3,2,0,1:T(8,128)}), f32[2,16,16,2048]{3,2,0,1:T(8,128)}, u32[]{:S(2)}, u32[]{:S(2)}) async-start(f32[2,16,16,2048]{3,2,0,1:T(8,128)} %pad_maximum_fusion.6), calls=%async_computation.5 | async-start | bytes 8388608 | tf_op jit(solution)/shard_map/all_to_all | solution.py:174
  103.0 42.3 %all-gather.5.cloned.1.call-start = ((), (), s32[]{:S(2)}) async-start(), calls=%async_computation.10 | async-start | bytes 1179648 | tf_op jit(solution)/shard_map/all_gather | solution.py:154
  105.2 68.7 %copy-start.12 = (f32[2,128,2,128]{3,2,1,0:T(2,128)}, f32[2,128,2,128]{3,2,1,0:T(2,128)S(1)}, u32[]{:S(2)}) copy-start(f32[2,128,2,128]{3,2,1,0:T(2,128)S(1)} %reshape.369) | copy-start | bytes 786436
  105.3 53.1 %copy-start.22 = (s32[2048]{0:T(1024)}, s32[2048]{0:T(1024)S(1)}, u32[]{:S(2)}) copy-start(s32[2048]{0:T(1024)S(1)} %add_select_fusion.3) | copy-start | bytes 24580
  105.3 53.0 %copy-start.24 = (s32[256]{0:T(256)}, s32[256]{0:T(256)S(1)}, u32[]{:S(2)}) copy-start(s32[256]{0:T(256)S(1)} %add_bitcast_fusion) | copy-start | bytes 3076
  145.3 6.3 copy-start.26
  164.7 7.1 copy-start.1
  171.8 2.0 copy-start.3
  187.4 55.6 %all-to-all-start.6 = ((f32[2,2,128,2048]{3,0,1,2:T(2,128)}), f32[2,2,128,2048]{3,0,1,2:T(2,128)}, u32[]{:S(2)}, u32[]{:S(2)}) async-start(f32[2,2,128,2048]{3,0,1,2:T(2,128)} %copy.198), calls=%async_computation.6 | async-start | bytes 8388608 | tf_op jit(solution)/shard_map/all_to_all | solution.py:184
  367.0 346.0 %copy-start.6 = (f32[1,128,4096]{2,1,0:T(8,128)}, f32[1,128,4096]{2,1,0:T(8,128)S(1)}, u32[]{:S(2)}) copy-start(f32[1,128,4096]{2,1,0:T(8,128)S(1)} %get-tuple-element.25) | copy-start | bytes 6291460
  505.9 8.3 %copy-start.2 = (f32[2,2,128,2048]{2,3,0,1:T(8,128)S(1)}, f32[2,2,128,2048]{2,3,0,1:T(8,128)}, u32[]{:S(2)}) copy-start(f32[2,2,128,2048]{2,3,0,1:T(8,128)} %fusion.39) | copy-start | bytes 12582916
  505.9 8.3 %copy-start.4 = (f32[2,2,128,2048]{2,3,0,1:T(8,128)S(1)}, f32[2,2,128,2048]{2,3,0,1:T(8,128)}, u32[]{:S(2)}) copy-start(f32[2,2,128,2048]{2,3,0,1:T(8,128)} %copy-done.3) | copy-start | bytes 12582916
  514.2 5.4 copy-start.13
  678.1 4.8 copy-start.23
  678.1 31.1 %all-to-all-start.3 = ((f32[8,16,4096]{2,1,0:T(8,128)}), f32[8,16,4096]{2,1,0:T(8,128)}, u32[]{:S(2)}, u32[]{:S(2)}) async-start(f32[8,16,4096]{2,1,0:T(8,128)} %copy.183), calls=%async_computation.3 | async-start | bytes 4194304 | tf_op jit(solution)/shard_map/all_to_all | solution.py:189
  682.6 76.5 %reduce-scatter.2.cloned.1.call-start = ((), (), s32[]{:S(2)}) async-start(), calls=%async_computation.9 | async-start | bytes 1179648 | tf_op jit(solution)/shard_map/reduce_scatter | solution.py:218
  682.9 5.8 copy-start.25
  688.6 20.6 %copy-start.11 = (bf16[1,128,4096]{2,1,0:T(8,128)(2,1)S(1)}, bf16[1,128,4096]{2,1,0:T(8,128)(2,1)}, u32[]{:S(2)}) copy-start(bf16[1,128,4096]{2,1,0:T(8,128)(2,1)} %param.9) | copy-start | bytes 3145732
  709.2 3.7 copy-start.8
  712.9 1.4 copy-start.9
  712.9 2.7 copy-start.27
  714.4 7.6 collective-permute-start.1
  715.7 12.3 %slice-start = ((s8[6684672]{0:T(1024)(128)(4,1)}), s8[2490368]{0:T(1024)(128)(4,1)S(1)}, s32[]{:S(2)}) async-start(s8[6684672]{0:T(1024)(128)(4,1)} %bitcast.246), calls=%async_computation.12 | async-start | bytes 4980736
  721.9 64.7 %all-gather.7.cloned.1.call-start = ((), (), s32[]{:S(2)}) async-start(), calls=%async_computation.11 | async-start | bytes 1769472 | tf_op jit(solution)/shard_map/all_gather | solution.py:215
  722.0 5.9 slice-start.1
  722.0 7.2 copy-start.7
  722.0 7.2 copy-start.16
  722.0 7.2 copy-start.18
  722.1 7.1 copy-start.20
  739.1 73.0 %collective-permute-start.2 = (bf16[3,128,4096]{2,1,0:T(8,128)(2,1)}, bf16[3,128,4096]{2,1,0:T(8,128)(2,1)S(1)}, u32[]{:S(2)}, u32[]{:S(2)}) collective-permute-start(bf16[3,128,4096]{2,1,0:T(8,128)(2,1)} %get-tuple-element.31), channel_id=1, source_target_pairs={{1,0},{2,1},{3,2},{5,4},{6,5},{7,6},{9,8},{10,9},{11,10},{13,12},{... | collective-permute-start | bytes 9437192 | tf_op jit(solution)/shard_map/ppermute | solution.py:13
Sparse Core Ops, SparseCore 0:
  105.7 39.5 all-gather.4
  722.0 37.0 reduce-scatter.1
  761.0 25.5 all-gather.6
